TPU v7x, 32 devices: a whole 2x2x4 slice. The times are simulated.
32 devices in a mesh: groups: 2 (over x), rows: 16 (over z, y, core).
Axes of the slice: x: 2, y: 2, z: 4, core: 2. Of those that a mesh axis runs over, the one named last changes fastest.
Arguments:
- tokens: bfloat16 [64, 256, 1024], P(('groups', 'rows')), parts along dimension 0, may hold values from -6 to 6
- peg_weight: float32 [3, 3, 1024], replicated, may hold values from -2 to 2
- peg_bias: float32 [1024], replicated, may hold values from -3 to 3
- norm_gain: float32 [1024], replicated, may hold values from 0.25 to 1.75
- norm_bias: float32 [1024], replicated, may hold values from -3 to 3
- qkv_weight: bfloat16 [1024, 3072], replicated, may hold values from -1 to 1
- qkv_bias: float32 [3072], replicated, may hold values from -3 to 3
- out_weight: bfloat16 [1024, 1024], replicated, may hold values from -0.1875 to 0.1875
- out_bias: float32 [1024], replicated, may hold values from -3 to 3
Outputs:
- result: bfloat16 [64, 256, 1024], P(('groups', 'rows')), parts along dimension 0
There are 2 independent parts, one for each index of `groups`. A program takes and returns all parts, laid end to end along the dimension named above; an argument that names none is the same for every part. Nothing has to cross between parts.
All inputs are finite; a program needn't handle non-finite values.
Results may differ from a plain program's by a relative error of at most 0.006.
Values may be sent and summed in bfloat16 or wider, within the bound.
No kernel may reach another device: no remote copies, remote signals or barrier semaphores. Data moves between devices by JAX's collectives and lax.ppermute only.
A program may use at most 64 MiB of HBM per device.

v0:
```python
import math
import jax
import jax.numpy as jnp
from jax import lax
from jax.sharding import PartitionSpec as P

HEADS = 16
DH = 64
ROW_HEADS = 8


def with_halo(value, sides, width):
    for axis, dim in sides:
        devices, length = (lax.axis_size(axis), value.shape[dim])
        up = [(i, (i + 1) % devices) for i in range(devices - 1)]
        down = [(j, i) for i, j in up]
        last = lax.slice_in_dim(value, length - width, length, axis=dim)
        leading = lax.slice_in_dim(value, 0, width, axis=dim)
        before = lax.ppermute(last, axis, up)
        after = lax.ppermute(leading, axis, down)
        value = jnp.concatenate([before, value, after], axis=dim)
    return value


def convolve(padded, peg_weight, peg_bias, count_rows, count_cols):
    total = padded[1 : count_rows + 1, 1 : count_cols + 1, :].astype(jnp.float32) + peg_bias
    for offset_row in range(3):
        for offset_col in range(3):
            piece = padded[
                offset_row : offset_row + count_rows, offset_col : offset_col + count_cols, :
            ]
            total = total + piece.astype(jnp.float32) * peg_weight[offset_row, offset_col]
    return total.astype(jnp.bfloat16)


def layer_norm(mixed, norm_gain, norm_bias):
    values = mixed.astype(jnp.float32)
    center = jnp.mean(values, axis=-1, keepdims=True)
    spread = jnp.mean((values - center) ** 2, axis=-1, keepdims=True)
    return ((values - center) * lax.rsqrt(spread + 1e-06) * norm_gain + norm_bias).astype(
        jnp.bfloat16
    )


def project_three(normed, qkv_weight, qkv_bias, first_col, last_col):
    model = normed.shape[-1]
    flat_rows = normed.reshape(-1, model)
    outputs = []
    for part_index in range(3):
        lower = part_index * model + first_col
        upper = part_index * model + last_col
        projected = (
            jnp.dot(flat_rows, qkv_weight[:, lower:upper], preferred_element_type=jnp.float32)
            + qkv_bias[lower:upper]
        )
        outputs.append(
            projected.astype(jnp.bfloat16).reshape(normed.shape[:-1] + (last_col - first_col,))
        )
    return (outputs[0], outputs[1], outputs[2])


def attend_heads(
    query_all, key_all, value_all, head_count, softmax_divisor, scoring_equation, mixing_equation
):
    outputs = []
    for head_index in range(head_count):
        lower = head_index * DH
        query_rows = query_all[..., lower : lower + DH]
        key_operand = key_all[..., lower : lower + DH]
        value_operand = value_all[..., lower : lower + DH]
        attention_logits = (
            jnp.einsum(
                scoring_equation, query_rows, key_operand, preferred_element_type=jnp.float32
            )
            * softmax_divisor
        )
        highest = jnp.max(attention_logits, axis=-1, keepdims=True)
        attention_weights = jnp.exp(attention_logits - highest)
        attention_weights = (
            attention_weights / jnp.sum(attention_weights, axis=-1, keepdims=True)
        ).astype(jnp.bfloat16)
        outputs.append(
            jnp.einsum(
                mixing_equation,
                attention_weights,
                value_operand,
                preferred_element_type=jnp.float32,
            ).astype(jnp.bfloat16)
        )
    return jnp.concatenate(outputs, axis=-1)


def on_device(
    tokens, peg_weight, peg_bias, norm_gain, norm_bias, qkv_weight, qkv_bias, out_weight, out_bias
):
    bands = tokens.shape[0]
    width = tokens.shape[1]
    model = tokens.shape[2]
    height = bands * lax.axis_size("rows")
    row_features = ROW_HEADS * DH
    col_count = HEADS - ROW_HEADS
    padded = with_halo(tokens, (("rows", 0),), 1)
    padded = jnp.pad(padded, ((0, 0), (1, 1), (0, 0)))
    mixed = convolve(padded, peg_weight, peg_bias, bands, width)
    normed = layer_norm(mixed, norm_gain, norm_bias)
    row_query, row_key, row_value = project_three(normed, qkv_weight, qkv_bias, 0, row_features)
    arrived = lax.all_to_all(normed, "rows", split_axis=1, concat_axis=0, tiled=True)
    col_query, col_key, col_value = project_three(
        arrived, qkv_weight, qkv_bias, row_features, model
    )
    tau_row = math.log(width) / (math.log(16.0) * math.sqrt(DH))
    tau_col = math.log(height) / (math.log(16.0) * math.sqrt(DH))
    row_heads = attend_heads(
        row_query, row_key, row_value, ROW_HEADS, tau_row, "bld,bmd->blm", "blm,bmd->bld"
    )
    col_heads = attend_heads(
        col_query, col_key, col_value, col_count, tau_col, "lbd,mbd->blm", "blm,mbd->lbd"
    )
    returned = lax.all_to_all(col_heads, "rows", split_axis=0, concat_axis=1, tiled=True)
    attended = jnp.concatenate([row_heads, returned], axis=2).reshape(bands * width, model)
    result = (
        mixed.reshape(bands * width, model).astype(jnp.float32)
        + jnp.dot(attended, out_weight, preferred_element_type=jnp.float32)
        + out_bias
    )
    return result.astype(jnp.bfloat16).reshape(bands, width, model)


def solution(mesh):
    placed = (P(("groups", "rows"), None, None), P(), P(), P(), P(), P(), P(), P(), P())
    return jax.shard_map(
        on_device,
        mesh=mesh,
        in_specs=placed,
        out_specs=P(("groups", "rows"), None, None),
        check_vma=False,
    )
```

profile of v0, /device:TPU:0, one launch (start us, length us, event | category | flops | bytes accessed | tf_op | source)
XLA Modules:
  0.0 165.9 jit_solution(17638637918727739005)
XLA Ops:
  1.4 2.4 %collective-permute-start = (bf16[1,256,1024]{2,1,0:T(8,128)(2,1)S(1)}, bf16[1,256,1024]{2,1,0:T(8,128)(2,1)S(1)}, u32[]{:S(2)}, u32[]{:S(2)}) collective-permute-start(bf16[1,256,1024]{2,1,0:T(8,128)(2,1)S(1)} %get-tuple-element.7), channel_id=1, source_target_pairs={{0,1},{1,2},{2,3},{3,4},{4,5},{5,6},{6,7},{7,8},{8,9},{9,10},{10,1... | collective-permute-start | bytes 1572872 | tf_op jit(solution)/shard_map/ppermute | solution.py:19
  5.3 4.4 %collective-permute-done.1 = bf16[1,256,1024]{2,1,0:T(8,128)(2,1)S(1)} collective-permute-done((bf16[1,256,1024]{2,1,0:T(8,128)(2,1)S(1)}, bf16[1,256,1024]{2,1,0:T(8,128)(2,1)S(1)}, u32[]{:S(2)}, u32[]{:S(2)}) %collective-permute-start.1) | collective-permute-done | bytes 524320 | tf_op jit(solution)/shard_map/ppermute | solution.py:20
  10.5 2.6 %convert_reduce_fusion = (f32[2,256]{1,0:T(2,128)S(1)}, bf16[2,256,1024]{2,1,0:T(8,128)(2,1)S(1)}) fusion(f32[1024]{0:T(1024)S(1)} %bitcast.137, bf16[4,258,1024]{2,1,0:T(8,128)(2,1)S(1)} %fusion.21, f32[1024]{0:T(1024)S(1)} %bitcast.138, bf16[1,256,1024]{2,1,0:T(8,128)(2,1)S(1)} %collective-permute-done.1, bf16[2,256,1024]{2,1,0:T(8,128)(2,1)S(1)} %copy-done.1, ...), kind=kLoop, calls=%fused_computation.41 | loop fusion | flops 17300992 | bytes 9480192 | tf_op jit(solution)/shard_map/reduce_sum | solution.py:38
  14.0 3.1 %fusion.35 = bf16[512,512]{1,0:T(8,128)(2,1)} fusion(bf16[512,1024]{1,0:T(8,128)(2,1)S(1)} %bitcast.79, bf16[1024,3072]{1,0:T(8,128)(2,1)} %param.14, f32[512]{0:T(512)S(1)} %get-tuple-element.45), kind=kOutput, calls=%fused_computation.49 | convolution fusion | flops 537395200 | bytes 2623488 | tf_op jit(solution)/shard_map/dot_general | solution.py:53
  17.1 2.8 %fusion.34 = bf16[512,512]{1,0:T(8,128)(2,1)} fusion(bf16[512,1024]{1,0:T(8,128)(2,1)S(1)} %bitcast.80, bf16[1024,3072]{1,0:T(8,128)(2,1)} %param.14, f32[512]{0:T(512)S(1)} %get-tuple-element.46), kind=kOutput, calls=%fused_computation.48 | convolution fusion | flops 537395200 | bytes 2623488 | tf_op jit(solution)/shard_map/dot_general | solution.py:53
  28.7 2.1 %convolution_multiply_fusion.2 = f32[2,256,256]{1,2,0:T(8,128)} fusion(bf16[2,256,512]{2,1,0:T(8,128)(2,1)} %bitcast.91, bf16[2,256,512]{2,1,0:T(8,128)(2,1)} %bitcast.107), kind=kOutput, calls=%fused_computation.72 | convolution fusion | flops 16908288 | bytes 786432 | tf_op jit(solution)/shard_map/bld,bmd->blm/dot_general | solution.py:72
  32.9 2.7 %fusion.36 = bf16[512,512]{1,0:T(8,128)(2,1)} fusion(bf16[512,1024]{1,0:T(8,128)(2,1)S(1)} %bitcast.81, bf16[1024,3072]{1,0:T(8,128)(2,1)} %param.14, f32[512]{0:T(512)S(1)} %get-tuple-element.44), kind=kOutput, calls=%fused_computation.50 | convolution fusion | flops 537395200 | bytes 2623488 | tf_op jit(solution)/shard_map/dot_general | solution.py:53
  35.6 14.6 %all-to-all-start = ((bf16[2,256,1024]{2,0,1:T(2,128)(2,1)}), bf16[2,256,1024]{2,0,1:T(2,128)(2,1)}, u32[]{:S(2)}, u32[]{:S(2)}) async-start(bf16[2,256,1024]{2,0,1:T(2,128)(2,1)} %copy.367), calls=%async_computation | async-start | bytes 2097152 | tf_op jit(solution)/shard_map/all_to_all | solution.py:107
  50.3 2.1 %convolution_convert_fusion.9 = bf16[2,256,64]{1,2,0:T(8,128)(2,1)} fusion(f32[2,256]{1,0:T(2,128)S(1)} %fusion.275, bf16[2,256,512]{2,1,0:T(8,128)(2,1)} %bitcast.139, f32[2,256,256]{1,2,0:T(8,128)} %convolution_multiply_fusion.1), kind=kOutput, calls=%fused_computation.119 | convolution fusion | flops 17203968 | bytes 1247232 | tf_op jit(solution)/shard_map/blm,bmd->bld/dot_general | solution.py:83
  52.4 2.2 %convolution_convert_fusion.10 = bf16[2,256,64]{1,2,0:T(8,128)(2,1)} fusion(f32[2,256]{1,0:T(2,128)S(1)} %fusion.270, bf16[2,256,512]{2,1,0:T(8,128)(2,1)} %bitcast.140, f32[2,256,256]{1,2,0:T(8,128)} %convolution_multiply_fusion.2), kind=kOutput, calls=%fused_computation.120 | convolution fusion | flops 17203968 | bytes 1247232 | tf_op jit(solution)/shard_map/blm,bmd->bld/dot_general | solution.py:83
  58.6 2.2 %convolution_convert_fusion.11 = bf16[2,256,64]{1,2,0:T(8,128)(2,1)} fusion(f32[2,256]{1,0:T(2,128)S(1)} %fusion.265, bf16[2,256,512]{2,1,0:T(8,128)(2,1)} %bitcast.141, f32[2,256,256]{1,2,0:T(8,128)} %convolution_multiply_fusion.3), kind=kOutput, calls=%fused_computation.121 | convolution fusion | flops 17203968 | bytes 1247232 | tf_op jit(solution)/shard_map/blm,bmd->bld/dot_general | solution.py:83
  60.7 2.1 %convolution_multiply_fusion.4 = f32[2,256,256]{1,2,0:T(8,128)} fusion(bf16[2,256,512]{2,1,0:T(8,128)(2,1)} %bitcast.94, bf16[2,256,512]{2,1,0:T(8,128)(2,1)} %bitcast.110), kind=kOutput, calls=%fused_computation.74 | convolution fusion | flops 16908288 | bytes 786432 | tf_op jit(solution)/shard_map/bld,bmd->blm/dot_general | solution.py:72
  62.8 2.2 %convolution_convert_fusion.12 = bf16[2,256,64]{1,2,0:T(8,128)(2,1)} fusion(f32[2,256]{1,0:T(2,128)S(1)} %fusion.260, bf16[2,256,512]{2,1,0:T(8,128)(2,1)} %bitcast.142, f32[2,256,256]{1,2,0:T(8,128)} %convolution_multiply_fusion.4), kind=kOutput, calls=%fused_computation.122 | convolution fusion | flops 17203968 | bytes 1247232 | tf_op jit(solution)/shard_map/blm,bmd->bld/dot_general | solution.py:83
  67.0 2.2 %convolution_convert_fusion.13 = bf16[2,256,64]{1,2,0:T(8,128)(2,1)} fusion(f32[2,256]{1,0:T(2,128)S(1)} %fusion.255, bf16[2,256,512]{2,1,0:T(8,128)(2,1)} %bitcast.143, f32[2,256,256]{1,2,0:T(8,128)} %convolution_multiply_fusion.5), kind=kOutput, calls=%fused_computation.123 | convolution fusion | flops 17203968 | bytes 1247232 | tf_op jit(solution)/shard_map/blm,bmd->bld/dot_general | solution.py:83
  74.9 2.3 %fusion.39 = bf16[512,512]{1,0:T(8,128)(2,1)S(1)} fusion(bf16[512,1024]{1,0:T(8,128)(2,1)S(1)} %bitcast.119, bf16[1024,3072]{1,0:T(8,128)(2,1)} %param.14, f32[512]{0:T(512)S(1)} %get-tuple-element.47), kind=kOutput, calls=%fused_computation.53 | convolution fusion | flops 537395200 | bytes 2623488 | tf_op jit(solution)/shard_map/dot_general | solution.py:53
  107.3 2.2 %fusion.37 = bf16[512,512]{1,0:T(8,128)(2,1)S(1)} fusion(bf16[512,1024]{1,0:T(8,128)(2,1)} %bitcast.121, bf16[1024,3072]{1,0:T(8,128)(2,1)} %param.14, f32[512]{0:T(512)S(1)} %get-tuple-element.43), kind=kOutput, calls=%fused_computation.51 | convolution fusion | flops 537395200 | bytes 2623488 | tf_op jit(solution)/shard_map/dot_general | solution.py:53
  125.3 2.1 %concatenate.45 = bf16[32,16,512]{2,0,1:T(8,128)(2,1)} concatenate(bf16[32,16,64]{2,0,1:T(8,128)(2,1)S(1)} %fusion.72, bf16[32,16,64]{2,0,1:T(8,128)(2,1)} %fusion.73, bf16[32,16,64]{2,0,1:T(8,128)(2,1)} %fusion.74, bf16[32,16,64]{2,0,1:T(8,128)(2,1)} %fusion.75, bf16[32,16,64]{2,0,1:T(8,128)(2,1)} %fusion.76, bf16[32,16,64]{2,0,1:T(8,128)(2,1)} %fusion.77, ...), dimensions={2} | concatenate | bytes 1048576 | tf_op jit(solution)/shard_map/concatenate | solution.py:90
  127.4 2.2 %copy.402 = bf16[32,16,512]{2,1,0:T(8,128)(2,1)} copy(bf16[32,16,512]{2,0,1:T(8,128)(2,1)} %concatenate.45) | data formatting | bytes 1048576 | tf_op jit(solution)/shard_map/concatenate | solution.py:90
  129.6 6.9 %all-to-all-start.1 = ((bf16[32,16,512]{2,1,0:T(8,128)(2,1)}), bf16[32,16,512]{2,1,0:T(8,128)(2,1)}, u32[]{:S(2)}, u32[]{:S(2)}) async-start(bf16[32,16,512]{2,1,0:T(8,128)(2,1)} %copy.402), calls=%async_computation.1 | async-start | bytes 1048576 | tf_op jit(solution)/shard_map/all_to_all | solution.py:119
  136.6 2.2 %convolution_convert_fusion.14 = bf16[2,256,64]{1,2,0:T(8,128)(2,1)} fusion(f32[2,256]{1,0:T(2,128)S(1)} %copy-done.16, bf16[2,256,512]{2,1,0:T(8,128)(2,1)} %bitcast.144, f32[2,256,256]{1,2,0:T(8,128)} %convolution_multiply_fusion.6), kind=kOutput, calls=%fused_computation.124 | convolution fusion | flops 17203968 | bytes 1247232 | tf_op jit(solution)/shard_map/blm,bmd->bld/dot_general | solution.py:83
  146.1 2.2 %convolution_convert_fusion.15 = bf16[2,256,64]{1,2,0:T(8,128)(2,1)} fusion(f32[2,256]{1,0:T(2,128)S(1)} %fusion.245, bf16[2,256,512]{2,1,0:T(8,128)(2,1)} %bitcast.145, f32[2,256,256]{1,2,0:T(8,128)} %convolution_multiply_fusion.7), kind=kOutput, calls=%fused_computation.125 | convolution fusion | flops 17203968 | bytes 1247232 | tf_op jit(solution)/shard_map/blm,bmd->bld/dot_general | solution.py:83
  153.3 2.1 %convolution_convert_fusion.8 = bf16[2,256,64]{1,2,0:T(8,128)(2,1)} fusion(f32[2,256]{1,0:T(2,128)S(1)} %fusion.280, bf16[2,256,512]{2,1,0:T(8,128)(2,1)} %bitcast.146, f32[2,256,256]{1,2,0:T(8,128)} %convolution_multiply_fusion), kind=kOutput, calls=%fused_computation.118 | convolution fusion | flops 17203968 | bytes 1247232 | tf_op jit(solution)/shard_map/blm,bmd->bld/dot_general | solution.py:83
  158.9 3.5 %concatenate.47 = bf16[512,1024]{1,0:T(8,128)(2,1)} concatenate(bf16[512,64]{1,0:T(8,128)(2,1)} %bitcast.128, bf16[512,64]{1,0:T(8,128)(2,1)} %bitcast.127, bf16[512,64]{1,0:T(8,128)(2,1)} %bitcast.126, bf16[512,64]{1,0:T(8,128)(2,1)} %bitcast.125, bf16[512,64]{1,0:T(8,128)(2,1)S(1)} %bitcast.124, bf16[512,64]{1,0:T(8,128)(2,1)S(1)} %bitcast.123, bf16[512,64]{1,0:T(8,128)(2,1)S(1)} %bitcast.122, ...), dimensions={1} | concatenate | bytes 2097152 | tf_op jit(solution)/shard_map/concatenate | solution.py:120
  162.4 3.5 %fusion.33 = bf16[512,1024]{1,0:T(8,128)(2,1)} fusion(bf16[2,256,1024]{2,1,0:T(8,128)(2,1)S(1)} %get-tuple-element.6, bf16[512,1024]{1,0:T(8,128)(2,1)} %concatenate.47, bf16[1024,1024]{1,0:T(8,128)(2,1)S(1)} %copy-done, f32[1024]{0:T(1024)S(1)} %copy-done.12), kind=kOutput, calls=%fused_computation.38 | convolution fusion | flops 1075838976 | bytes 5246976 | tf_op jit(solution)/shard_map/dot_general | solution.py:123
  (99 shorter events, 88.7 us)
Async XLA Ops:
  0.0 162.4 %copy-start = (bf16[1024,1024]{1,0:T(8,128)(2,1)S(1)}, bf16[1024,1024]{1,0:T(8,128)(2,1)}, u32[]{:S(2)}) copy-start(bf16[1024,1024]{1,0:T(8,128)(2,1)} %param.16) | copy-start | bytes 6291460
  0.0 9.7 %copy-start.1 = (bf16[2,256,1024]{2,1,0:T(8,128)(2,1)S(1)}, bf16[2,256,1024]{2,1,0:T(8,128)(2,1)}, u32[]{:S(2)}) copy-start(bf16[2,256,1024]{2,1,0:T(8,128)(2,1)} %param.9) | copy-start | bytes 3145732
  0.0 5.1 %copy-start.8 = (f32[3072]{0:T(1024)S(1)}, f32[3072]{0:T(1024)}, u32[]{:S(2)}) copy-start(f32[3072]{0:T(1024)} %param.15) | copy-start | bytes 36868
  0.0 5.2 %copy-start.7 = (f32[3,3,1024]{2,1,0:T(4,128)S(1)}, f32[3,3,1024]{2,1,0:T(4,128)}, u32[]{:S(2)}) copy-start(f32[3,3,1024]{2,1,0:T(4,128)} %param.10) | copy-start | bytes 110596
  1.4 3.9 %collective-permute-start = (bf16[1,256,1024]{2,1,0:T(8,128)(2,1)S(1)}, bf16[1,256,1024]{2,1,0:T(8,128)(2,1)S(1)}, u32[]{:S(2)}, u32[]{:S(2)}) collective-permute-start(bf16[1,256,1024]{2,1,0:T(8,128)(2,1)S(1)} %get-tuple-element.7), channel_id=1, source_target_pairs={{0,1},{1,2},{2,3},{3,4},{4,5},{5,6},{6,7},{7,8},{8,9},{9,10},{10,1... | collective-permute-start | bytes 1572872 | tf_op jit(solution)/shard_map/ppermute | solution.py:19
  3.8 5.9 %collective-permute-start.1 = (bf16[1,256,1024]{2,1,0:T(8,128)(2,1)S(1)}, bf16[1,256,1024]{2,1,0:T(8,128)(2,1)S(1)}, u32[]{:S(2)}, u32[]{:S(2)}) collective-permute-start(bf16[1,256,1024]{2,1,0:T(8,128)(2,1)S(1)} %get-tuple-element.8), channel_id=1, source_target_pairs={{1,0},{2,1},{3,2},{4,3},{5,4},{6,5},{7,6},{8,7},{9,8},{10,9},{11,1... | collective-permute-start | bytes 1572872 | tf_op jit(solution)/shard_map/ppermute | solution.py:20
  5.2 5.2 %copy-start.9 = (f32[1024]{0:T(1024)S(1)}, f32[1024]{0:T(1024)}, u32[]{:S(2)}) copy-start(f32[1024]{0:T(1024)} %param.11) | copy-start | bytes 12292
  10.4 3.1 %copy-start.10 = (f32[1024]{0:T(1024)S(1)}, f32[1024]{0:T(1024)}, u32[]{:S(2)}) copy-start(f32[1024]{0:T(1024)} %param.13) | copy-start | bytes 12292
  10.4 3.1 %copy-start.11 = (f32[1024]{0:T(1024)S(1)}, f32[1024]{0:T(1024)}, u32[]{:S(2)}) copy-start(f32[1024]{0:T(1024)} %param.12) | copy-start | bytes 12292
  14.0 5.9 %copy-start.2 = (bf16[2,256,1024]{2,1,0:T(8,128)(2,1)}, bf16[2,256,1024]{2,1,0:T(8,128)(2,1)S(1)}, u32[]{:S(2)}) copy-start(bf16[2,256,1024]{2,1,0:T(8,128)(2,1)S(1)} %add_convert_fusion) | copy-start | bytes 3145732
  26.7 4.2 %copy-start.3 = (bf16[2,256,1024]{2,1,0:T(8,128)(2,1)S(1)}, bf16[2,256,1024]{2,1,0:T(8,128)(2,1)}, u32[]{:S(2)}) copy-start(bf16[2,256,1024]{2,1,0:T(8,128)(2,1)} %copy-done.2) | copy-start | bytes 3145732
  35.6 37.6 %all-to-all-start = ((bf16[2,256,1024]{2,0,1:T(2,128)(2,1)}), bf16[2,256,1024]{2,0,1:T(2,128)(2,1)}, u32[]{:S(2)}, u32[]{:S(2)}) async-start(bf16[2,256,1024]{2,0,1:T(2,128)(2,1)} %copy.367), calls=%async_computation | async-start | bytes 2097152 | tf_op jit(solution)/shard_map/all_to_all | solution.py:107
  74.9 4.3 %copy-start.4 = (bf16[16,2,16,1024]{3,2,1,0:T(8,128)(2,1)}, bf16[16,2,16,1024]{3,2,1,0:T(8,128)(2,1)S(1)}, u32[]{:S(2)}) copy-start(bf16[16,2,16,1024]{3,2,1,0:T(8,128)(2,1)S(1)} %copy.369) | copy-start | bytes 3145732
  111.9 6.1 %copy-start.13 = (f32[16,32]{1,0:T(8,128)S(1)}, f32[16,32]{1,0:T(8,128)}, u32[]{:S(2)}) copy-start(f32[16,32]{1,0:T(8,128)} %fusion.300) | copy-start | bytes 6148
  114.0 6.1 %copy-start.14 = (f32[16,32]{1,0:T(8,128)S(1)}, f32[16,32]{1,0:T(8,128)}, u32[]{:S(2)}) copy-start(f32[16,32]{1,0:T(8,128)} %fusion.295) | copy-start | bytes 6148
  120.0 4.0 %copy-start.15 = (f32[16,32]{1,0:T(8,128)S(1)}, f32[16,32]{1,0:T(8,128)}, u32[]{:S(2)}) copy-start(f32[16,32]{1,0:T(8,128)} %fusion.285) | copy-start | bytes 6148
  125.3 11.2 %copy-start.16 = (f32[2,256]{1,0:T(2,128)S(1)}, f32[2,256]{1,0:T(2,128)}, u32[]{:S(2)}) copy-start(f32[2,256]{1,0:T(2,128)} %fusion.250) | copy-start | bytes 6148
  127.4 11.3 %copy-start.5 = (bf16[2,256,64]{1,2,0:T(8,128)(2,1)S(1)}, bf16[2,256,64]{1,2,0:T(8,128)(2,1)}, u32[]{:S(2)}) copy-start(bf16[2,256,64]{1,2,0:T(8,128)(2,1)} %convolution_convert_fusion.9) | copy-start | bytes 196612
  127.4 11.4 %copy-start.6 = (bf16[2,256,64]{1,2,0:T(8,128)(2,1)S(1)}, bf16[2,256,64]{1,2,0:T(8,128)(2,1)}, u32[]{:S(2)}) copy-start(bf16[2,256,64]{1,2,0:T(8,128)(2,1)} %convolution_convert_fusion.10) | copy-start | bytes 196612
  129.6 27.4 %all-to-all-start.1 = ((bf16[32,16,512]{2,1,0:T(8,128)(2,1)}), bf16[32,16,512]{2,1,0:T(8,128)(2,1)}, u32[]{:S(2)}, u32[]{:S(2)}) async-start(bf16[32,16,512]{2,1,0:T(8,128)(2,1)} %copy.402), calls=%async_computation.1 | async-start | bytes 1048576 | tf_op jit(solution)/shard_map/all_to_all | solution.py:119
  155.4 7.0 %copy-start.12 = (f32[1024]{0:T(1024)S(1)}, f32[1024]{0:T(1024)}, u32[]{:S(2)}) copy-start(f32[1024]{0:T(1024)} %param.17) | copy-start | bytes 12292
where the time goes:
time: 168 us; the launch traced here: 166 us
  matrix products  105 us (62%)
  local copies, waits for them, and re-layouts  26.5 us (16%)
  starting transfers between devices  25.3 us (15%)
  waiting for transfers between devices  4.53 us (3%)
  other arithmetic  4.12 us (2%)
    dot_general x16, matrix products, attend_heads(): jnp.einsum(mixing_equation, attention_weights, value_operand, preferred_e...  31.9 us
    dot_general x16, matrix products, attend_heads(): jnp.einsum(scoring_equation, query_rows, key_operand, preferred_element_t...  30.3 us
    sub x16, matrix products, attend_heads(): attention_weights = jnp.exp(attention_logits - highest)  24.3 us
    dot_general x6, matrix products, project_three(): jnp.dot(flat_rows, qkv_weight[:, lower:upper], preferred_element_type=jnp...  15.1 us
    all_to_all x1, starting transfers between devices, on_device(): lax.all_to_all(normed, 'rows', split_axis=1, concat_axis=0, tiled=True)  14.6 us
    concatenate x9, local copies, waits for them, and re-layouts, on_device(): jnp.concatenate([row_heads, returned], axis=2).reshape(bands * width, model)  12.6 us
    all_to_all x1, starting transfers between devices, on_device(): lax.all_to_all(col_heads, 'rows', split_axis=0, concat_axis=1, tiled=True)  6.93 us
    ppermute x1, waiting for transfers between devices, with_halo(): after = lax.ppermute(leading, axis, down)  4.42 us
  transfers between devices with their start and end apart: 4, of which 2 were waited for; matrix products, arithmetic and copies ran while one was open for 26% of the time, Pallas kernels for 0%

commit v1 on v0

--- a/solution.py
+++ b/solution.py
@@ -1,3 +1,4 @@
+import functools
 import math
 import jax
 import jax.numpy as jnp
@@ -7,6 +8,26 @@
 HEADS = 16
 DH = 64
 ROW_HEADS = 8
+
+
+def turn_series_all_on(u_in, axis_id, d_out, dim_no):
+    tile_out, x_new = (lax.axis_size(axis_id), lax.axis_index(axis_id))
+    v_now = u_in.shape[d_out] // tile_out
+    current_value = jnp.roll(u_in, shift=-x_new * v_now, axis=d_out)
+    panels = [lax.slice_in_dim(current_value, 0, v_now, axis=d_out)]
+    q = 1
+    while q < tile_out:
+        inter = lax.slice_in_dim(current_value, q * v_now, (q + 1) * v_now, axis=d_out)
+        panels.append(
+            lax.ppermute(inter, axis_id, [(j0, (j0 + q) % tile_out) for j0 in range(tile_out)])
+        )
+        q = q + 1
+    y2 = jnp.concatenate(panels[::-1], axis=dim_no)
+    near = jnp.roll(y2, (x_new + 1) * panels[0].shape[dim_no], axis=dim_no)
+    return near
+
+
+end_the_boxes = functools.partial(turn_series_all_on, axis_id="rows", d_out=0, dim_no=1)
 
 
 def with_halo(value, sides, width):
@@ -116,7 +137,7 @@
     col_heads = attend_heads(
         col_query, col_key, col_value, col_count, tau_col, "lbd,mbd->blm", "blm,mbd->lbd"
     )
-    returned = lax.all_to_all(col_heads, "rows", split_axis=0, concat_axis=1, tiled=True)
+    returned = end_the_boxes(col_heads)
     attended = jnp.concatenate([row_heads, returned], axis=2).reshape(bands * width, model)
     result = (
         mixed.reshape(bands * width, model).astype(jnp.float32)

time: 168 us -> 236 us (1.40)
  starting transfers between devices: 25.3 us -> 58.9 us
  waiting for transfers between devices: 4.53 us -> 24.3 us
  local copies, waits for them, and re-layouts: 26.5 us -> 37 us
  other arithmetic: 4.12 us -> 7.74 us
    ppermute x0 -> x15, starting transfers between devices: none -> 39.9 us  [turn_series_all_on(): lax.ppermute(inter, axis_id, [(j0, (j0 + q) % tile_out) for j0 in range(t...]
    ppermute x0 -> x15, waiting for transfers between devices: none -> 20.2 us  [turn_series_all_on(): lax.ppermute(inter, axis_id, [(j0, (j0 + q) % tile_out) for j0 in range(t...]
    convert_element_type x0 -> x8, local copies, waits for them, and re-layouts: none -> 9.25 us  [attend_heads(): outputs.append(jnp.einsum(mixing_equation, attention_weights, value_opera...]
    all_to_all x1 -> x0, starting transfers between devices: 6.93 us -> none  [on_device(): lax.all_to_all(col_heads, 'rows', split_axis=0, concat_axis=1, tiled=True)]
    unnamed x34 -> x69, local copies, waits for them, and re-layouts: 0.08 us -> 4.29 us
    concatenate x9 -> x2, local copies, waits for them, and re-layouts: 12.6 us -> 9.58 us  [on_device(): jnp.concatenate([row_heads, returned], axis=2).reshape(bands * width, model)]
  transfers between devices with their start and end apart: 4 -> 18, of which waited for: 2 -> 11; matrix products, arithmetic and copies ran while one was open for 26% -> 16% of each run, Pallas kernels for 0% -> 0%
where the time goes in v1:
time: 236 us; the launch traced here: 233 us
  matrix products  104 us (44%)
  starting transfers between devices  58.9 us (25%)
  local copies, waits for them, and re-layouts  37 us (16%)
  waiting for transfers between devices  24.3 us (10%)
  other arithmetic  7.74 us (3%)
    ppermute x15, starting transfers between devices, turn_series_all_on(): lax.ppermute(inter, axis_id, [(j0, (j0 + q) % tile_out) for j0 in range(t...  39.9 us
    dot_general x16, matrix products, attend_heads(): jnp.einsum(mixing_equation, attention_weights, value_operand, preferred_e...  32.1 us
    dot_general x16, matrix products, attend_heads(): jnp.einsum(scoring_equation, query_rows, key_operand, preferred_element_t...  30.4 us
    sub x16, matrix products, attend_heads(): attention_weights = jnp.exp(attention_logits - highest)  24.3 us
    ppermute x15, waiting for transfers between devices, turn_series_all_on(): lax.ppermute(inter, axis_id, [(j0, (j0 + q) % tile_out) for j0 in range(t...  20.2 us
    dot_general x6, matrix products, project_three(): jnp.dot(flat_rows, qkv_weight[:, lower:upper], preferred_element_type=jnp...  15.1 us
    all_to_all x1, starting transfers between devices, on_device(): lax.all_to_all(normed, 'rows', split_axis=1, concat_axis=0, tiled=True)  14.6 us
    concatenate x2, local copies, waits for them, and re-layouts, on_device(): jnp.concatenate([row_heads, returned], axis=2).reshape(bands * width, model)  9.58 us
  transfers between devices with their start and end apart: 18, of which 11 were waited for; matrix products, arithmetic and copies ran while one was open for 16% of the time, Pallas kernels for 0%

profile of v1, /device:TPU:0, one launch (start us, length us, event | category | flops | bytes accessed | tf_op | source)
XLA Modules:
  0.0 232.6 jit_solution(14194647368896380502)
XLA Ops:
  0.0 2.4 %fusion.240 = (bf16[1,256,1024]{2,1,0:T(8,128)(2,1)}, bf16[1,256,1024]{2,1,0:T(8,128)(2,1)}) fusion(bf16[2,256,1024]{2,1,0:T(8,128)(2,1)} %param.9), kind=kLoop, calls=%fused_computation.276 | loop fusion | bytes 2097152 | tf_op jit(solution)/shard_map/slice | solution.py:38
  2.4 3.2 %collective-permute-start = (bf16[1,256,1024]{2,1,0:T(8,128)(2,1)}, bf16[1,256,1024]{2,1,0:T(8,128)(2,1)}, u32[]{:S(2)}, u32[]{:S(2)}) collective-permute-start(bf16[1,256,1024]{2,1,0:T(8,128)(2,1)} %get-tuple-element.7), channel_id=1, source_target_pairs={{0,1},{1,2},{2,3},{3,4},{4,5},{5,6},{6,7},{7,8},{8,9},{9,10},{10,1... | collective-permute-start | bytes 1572872 | tf_op jit(solution)/shard_map/ppermute | solution.py:40
  7.0 4.0 %collective-permute-done.1 = bf16[1,256,1024]{2,1,0:T(8,128)(2,1)} collective-permute-done((bf16[1,256,1024]{2,1,0:T(8,128)(2,1)}, bf16[1,256,1024]{2,1,0:T(8,128)(2,1)}, u32[]{:S(2)}, u32[]{:S(2)}) %collective-permute-start.1) | collective-permute-done | bytes 524320 | tf_op jit(solution)/shard_map/ppermute | solution.py:41
  12.9 3.6 %convert_reduce_fusion = (f32[2,256]{1,0:T(2,128)S(1)}, bf16[2,256,1024]{2,1,0:T(8,128)(2,1)S(1)}) fusion(f32[1024]{0:T(1024)S(1)} %bitcast.118, bf16[4,258,1024]{2,1,0:T(8,128)(2,1)S(1)} %fusion.21, f32[1024]{0:T(1024)S(1)} %bitcast.119, bf16[1,256,1024]{2,1,0:T(8,128)(2,1)} %collective-permute-done.1, bf16[2,256,1024]{2,1,0:T(8,128)(2,1)S(1)} %copy-done.2, ...), kind=kLoop, calls=%fused_computation.41 | loop fusion | flops 17300992 | bytes 9480192 | tf_op jit(solution)/shard_map/reduce_sum | solution.py:59
  17.4 3.1 %fusion.35 = bf16[512,512]{1,0:T(8,128)(2,1)} fusion(bf16[512,1024]{1,0:T(8,128)(2,1)S(1)} %bitcast.68, bf16[1024,3072]{1,0:T(8,128)(2,1)} %param.14, f32[512]{0:T(512)S(1)} %get-tuple-element.60), kind=kOutput, calls=%fused_computation.49 | convolution fusion | flops 537395200 | bytes 2623488 | tf_op jit(solution)/shard_map/dot_general | solution.py:74
  20.6 2.8 %fusion.34 = bf16[512,512]{1,0:T(8,128)(2,1)} fusion(bf16[512,1024]{1,0:T(8,128)(2,1)S(1)} %bitcast.69, bf16[1024,3072]{1,0:T(8,128)(2,1)} %param.14, f32[512]{0:T(512)S(1)} %get-tuple-element.61), kind=kOutput, calls=%fused_computation.48 | convolution fusion | flops 537395200 | bytes 2623488 | tf_op jit(solution)/shard_map/dot_general | solution.py:74
  43.2 2.8 %fusion.36 = bf16[512,512]{1,0:T(8,128)(2,1)} fusion(bf16[512,1024]{1,0:T(8,128)(2,1)S(1)} %bitcast.70, bf16[1024,3072]{1,0:T(8,128)(2,1)} %param.14, f32[512]{0:T(512)S(1)} %get-tuple-element.59), kind=kOutput, calls=%fused_computation.50 | convolution fusion | flops 537395200 | bytes 2623488 | tf_op jit(solution)/shard_map/dot_general | solution.py:74
  46.0 14.6 %all-to-all-start = ((bf16[2,256,1024]{2,0,1:T(2,128)(2,1)}), bf16[2,256,1024]{2,0,1:T(2,128)(2,1)}, u32[]{:S(2)}, u32[]{:S(2)}) async-start(bf16[2,256,1024]{2,0,1:T(2,128)(2,1)} %copy.343), calls=%async_computation | async-start | bytes 2097152 | tf_op jit(solution)/shard_map/all_to_all | solution.py:128
  77.3 2.2 convolution_convert_fusion.14
  87.5 2.3 fusion.39
  120.0 2.2 fusion.37
  143.5 4.4 %collective-permute-start.2 = (bf16[2,16,512]{2,0,1:T(2,128)(2,1)}, bf16[2,16,512]{2,0,1:T(2,128)(2,1)}, u32[]{:S(2)}, u32[]{:S(2)}) collective-permute-start(bf16[2,16,512]{2,0,1:T(2,128)(2,1)} %get-tuple-element.23), channel_id=1, source_target_pairs={{0,15},{1,0},{2,1},{3,2},{4,3},{5,4},{6,5},{7,6},{8,7},{9,8},{10,9... | collective-permute-start | bytes 98312 | tf_op jit(solution)/shard_map/ppermute | solution.py:22
  161.1 4.2 %collective-permute-start.3 = (bf16[2,16,512]{2,0,1:T(2,128)(2,1)}, bf16[2,16,512]{2,0,1:T(2,128)(2,1)S(1)}, u32[]{:S(2)}, u32[]{:S(2)}) collective-permute-start(bf16[2,16,512]{2,0,1:T(2,128)(2,1)} %get-tuple-element.22), channel_id=1, source_target_pairs={{0,14},{1,15},{2,0},{3,1},{4,2},{5,3},{6,4},{7,5},{8,6},{9,7},{10,... | collective-permute-start | bytes 98312 | tf_op jit(solution)/shard_map/ppermute | solution.py:22
  167.2 3.5 %collective-permute-done.4 = bf16[2,16,512]{2,0,1:T(2,128)(2,1)S(1)} collective-permute-done((bf16[2,16,512]{2,0,1:T(2,128)(2,1)}, bf16[2,16,512]{2,0,1:T(2,128)(2,1)S(1)}, u32[]{:S(2)}, u32[]{:S(2)}) %collective-permute-start.4) | collective-permute-done | bytes 32800 | tf_op jit(solution)/shard_map/ppermute | solution.py:22
  172.6 2.2 collective-permute-done.5
  174.8 2.6 %collective-permute-start.6 = (bf16[2,16,512]{2,0,1:T(2,128)(2,1)}, bf16[2,16,512]{2,0,1:T(2,128)(2,1)S(1)}, u32[]{:S(2)}, u32[]{:S(2)}) collective-permute-start(bf16[2,16,512]{2,0,1:T(2,128)(2,1)} %get-tuple-element.19), channel_id=1, source_target_pairs={{0,11},{1,12},{2,13},{3,14},{4,15},{5,0},{6,1},{7,2},{8,3},{9,4},{... | collective-permute-start | bytes 98312 | tf_op jit(solution)/shard_map/ppermute | solution.py:22
  179.3 5.2 %collective-permute-start.7 = (bf16[2,16,512]{2,0,1:T(2,128)(2,1)}, bf16[2,16,512]{2,0,1:T(2,128)(2,1)S(1)}, u32[]{:S(2)}, u32[]{:S(2)}) collective-permute-start(bf16[2,16,512]{2,0,1:T(2,128)(2,1)} %get-tuple-element.18), channel_id=1, source_target_pairs={{0,10},{1,11},{2,12},{3,13},{4,14},{5,15},{6,0},{7,1},{8,2},{9,3},... | collective-permute-start | bytes 98312 | tf_op jit(solution)/shard_map/ppermute | solution.py:22
  186.4 3.8 %collective-permute-start.8 = (bf16[2,16,512]{2,0,1:T(2,128)(2,1)}, bf16[2,16,512]{2,0,1:T(2,128)(2,1)S(1)}, u32[]{:S(2)}, u32[]{:S(2)}) collective-permute-start(bf16[2,16,512]{2,0,1:T(2,128)(2,1)} %get-tuple-element.17), channel_id=1, source_target_pairs={{0,9},{1,10},{2,11},{3,12},{4,13},{5,14},{6,15},{7,0},{8,1},{9,2},... | collective-permute-start | bytes 98312 | tf_op jit(solution)/shard_map/ppermute | solution.py:22
  192.1 4.6 %collective-permute-start.9 = (bf16[2,16,512]{2,0,1:T(2,128)(2,1)}, bf16[2,16,512]{2,0,1:T(2,128)(2,1)S(1)}, u32[]{:S(2)}, u32[]{:S(2)}) collective-permute-start(bf16[2,16,512]{2,0,1:T(2,128)(2,1)} %get-tuple-element.16), channel_id=1, source_target_pairs={{0,8},{1,9},{2,10},{3,11},{4,12},{5,13},{6,14},{7,15},{8,0},{9,1},... | collective-permute-start | bytes 98312 | tf_op jit(solution)/shard_map/ppermute | solution.py:22
  198.8 2.7 %collective-permute-start.10 = (bf16[2,16,512]{2,0,1:T(2,128)(2,1)}, bf16[2,16,512]{2,0,1:T(2,128)(2,1)S(1)}, u32[]{:S(2)}, u32[]{:S(2)}) collective-permute-start(bf16[2,16,512]{2,0,1:T(2,128)(2,1)} %get-tuple-element.15), channel_id=1, source_target_pairs={{0,7},{1,8},{2,9},{3,10},{4,11},{5,12},{6,13},{7,14},{8,15},{9,0},... | collective-permute-start | bytes 98312 | tf_op jit(solution)/shard_map/ppermute | solution.py:22
  203.4 5.2 %collective-permute-start.11 = (bf16[2,16,512]{2,0,1:T(2,128)(2,1)}, bf16[2,16,512]{2,0,1:T(2,128)(2,1)S(1)}, u32[]{:S(2)}, u32[]{:S(2)}) collective-permute-start(bf16[2,16,512]{2,0,1:T(2,128)(2,1)} %get-tuple-element.14), channel_id=1, source_target_pairs={{0,6},{1,7},{2,8},{3,9},{4,10},{5,11},{6,12},{7,13},{8,14},{9,15},... | collective-permute-start | bytes 98312 | tf_op jit(solution)/shard_map/ppermute | solution.py:22
  210.5 3.8 %collective-permute-start.12 = (bf16[2,16,512]{2,0,1:T(2,128)(2,1)}, bf16[2,16,512]{2,0,1:T(2,128)(2,1)S(1)}, u32[]{:S(2)}, u32[]{:S(2)}) collective-permute-start(bf16[2,16,512]{2,0,1:T(2,128)(2,1)} %get-tuple-element.13), channel_id=1, source_target_pairs={{0,5},{1,6},{2,7},{3,8},{4,9},{5,10},{6,11},{7,12},{8,13},{9,14},{... | collective-permute-start | bytes 98312 | tf_op jit(solution)/shard_map/ppermute | solution.py:22
  220.8 8.1 %concatenate.31 = bf16[2,256,1024]{2,0,1:T(2,128)(2,1)} concatenate(bf16[2,256,64]{2,0,1:T(2,128)(2,1)} %copy.378, bf16[2,256,64]{2,0,1:T(2,128)(2,1)} %copy.379, bf16[2,256,64]{2,0,1:T(2,128)(2,1)} %copy.380, bf16[2,256,64]{2,0,1:T(2,128)(2,1)} %copy.381, bf16[2,256,64]{2,0,1:T(2,128)(2,1)S(1)} %copy.382, bf16[2,256,64]{2,0,1:T(2,128)(2,1)S(1)} %copy.383, ...), dimensions={2} | concatenate | bytes 2097152 | tf_op jit(solution)/shard_map/concatenate | solution.py:141
  230.4 2.2 fusion.33
  (165 shorter events, 136.5 us)
Async XLA Ops:
  0.0 230.4 %copy-start = (bf16[1024,1024]{1,0:T(8,128)(2,1)S(1)}, bf16[1024,1024]{1,0:T(8,128)(2,1)}, u32[]{:S(2)}) copy-start(bf16[1024,1024]{1,0:T(8,128)(2,1)} %param.16) | copy-start | bytes 6291460
  0.0 11.0 %copy-start.1 = (bf16[2,256,1024]{2,1,0:T(8,128)(2,1)S(1)}, bf16[2,256,1024]{2,1,0:T(8,128)(2,1)}, u32[]{:S(2)}) copy-start(bf16[2,256,1024]{2,1,0:T(8,128)(2,1)} %param.9) | copy-start | bytes 3145732
  2.4 4.6 %collective-permute-start = (bf16[1,256,1024]{2,1,0:T(8,128)(2,1)}, bf16[1,256,1024]{2,1,0:T(8,128)(2,1)}, u32[]{:S(2)}, u32[]{:S(2)}) collective-permute-start(bf16[1,256,1024]{2,1,0:T(8,128)(2,1)} %get-tuple-element.7), channel_id=1, source_target_pairs={{0,1},{1,2},{2,3},{3,4},{4,5},{5,6},{6,7},{7,8},{8,9},{9,10},{10,1... | collective-permute-start | bytes 1572872 | tf_op jit(solution)/shard_map/ppermute | solution.py:40
  5.6 5.5 %collective-permute-start.1 = (bf16[1,256,1024]{2,1,0:T(8,128)(2,1)}, bf16[1,256,1024]{2,1,0:T(8,128)(2,1)}, u32[]{:S(2)}, u32[]{:S(2)}) collective-permute-start(bf16[1,256,1024]{2,1,0:T(8,128)(2,1)} %get-tuple-element.8), channel_id=1, source_target_pairs={{1,0},{2,1},{3,2},{4,3},{5,4},{6,5},{7,6},{8,7},{9,8},{10,9},{11,1... | collective-permute-start | bytes 1572872 | tf_op jit(solution)/shard_map/ppermute | solution.py:41
  46.0 39.9 %all-to-all-start = ((bf16[2,256,1024]{2,0,1:T(2,128)(2,1)}), bf16[2,256,1024]{2,0,1:T(2,128)(2,1)}, u32[]{:S(2)}, u32[]{:S(2)}) async-start(bf16[2,256,1024]{2,0,1:T(2,128)(2,1)} %copy.343), calls=%async_computation | async-start | bytes 2097152 | tf_op jit(solution)/shard_map/all_to_all | solution.py:128
  138.0 9.9 %copy-start.18 = (f32[2,256]{1,0:T(2,128)S(1)}, f32[2,256]{1,0:T(2,128)}, u32[]{:S(2)}) copy-start(f32[2,256]{1,0:T(2,128)} %fusion.247) | copy-start | bytes 6148
  140.2 10.0 %copy-start.7 = (bf16[2,256,64]{1,2,0:T(8,128)(2,1)S(1)}, bf16[2,256,64]{1,2,0:T(8,128)(2,1)}, u32[]{:S(2)}) copy-start(bf16[2,256,64]{1,2,0:T(8,128)(2,1)} %convolution_convert_fusion.9) | copy-start | bytes 196612
  140.2 10.1 %copy-start.8 = (bf16[2,256,64]{1,2,0:T(8,128)(2,1)S(1)}, bf16[2,256,64]{1,2,0:T(8,128)(2,1)}, u32[]{:S(2)}) copy-start(bf16[2,256,64]{1,2,0:T(8,128)(2,1)} %convolution_convert_fusion.10) | copy-start | bytes 196612
  143.5 17.5 %collective-permute-start.2 = (bf16[2,16,512]{2,0,1:T(2,128)(2,1)}, bf16[2,16,512]{2,0,1:T(2,128)(2,1)}, u32[]{:S(2)}, u32[]{:S(2)}) collective-permute-start(bf16[2,16,512]{2,0,1:T(2,128)(2,1)} %get-tuple-element.23), channel_id=1, source_target_pairs={{0,15},{1,0},{2,1},{3,2},{4,3},{5,4},{6,5},{7,6},{8,7},{9,8},{10,9... | collective-permute-start | bytes 98312 | tf_op jit(solution)/shard_map/ppermute | solution.py:22
  159.4 57.0 %collective-permute-start.16 = (bf16[2,16,512]{2,0,1:T(2,128)(2,1)}, bf16[2,16,512]{2,0,1:T(2,128)(2,1)S(1)}, u32[]{:S(2)}, u32[]{:S(2)}) collective-permute-start(bf16[2,16,512]{2,0,1:T(2,128)(2,1)} %get-tuple-element.9), channel_id=1, source_target_pairs={{0,1},{1,2},{2,3},{3,4},{4,5},{5,6},{6,7},{7,8},{8,9},{9,10},{10,1... | collective-permute-start | bytes 98312 | tf_op jit(solution)/shard_map/ppermute | solution.py:22
  159.4 56.9 %collective-permute-start.15 = (bf16[2,16,512]{2,0,1:T(2,128)(2,1)}, bf16[2,16,512]{2,0,1:T(2,128)(2,1)S(1)}, u32[]{:S(2)}, u32[]{:S(2)}) collective-permute-start(bf16[2,16,512]{2,0,1:T(2,128)(2,1)} %get-tuple-element.10), channel_id=1, source_target_pairs={{0,2},{1,3},{2,4},{3,5},{4,6},{5,7},{6,8},{7,9},{8,10},{9,11},{10,... | collective-permute-start | bytes 98312 | tf_op jit(solution)/shard_map/ppermute | solution.py:22
  159.4 56.9 %collective-permute-start.14 = (bf16[2,16,512]{2,0,1:T(2,128)(2,1)}, bf16[2,16,512]{2,0,1:T(2,128)(2,1)S(1)}, u32[]{:S(2)}, u32[]{:S(2)}) collective-permute-start(bf16[2,16,512]{2,0,1:T(2,128)(2,1)} %get-tuple-element.11), channel_id=1, source_target_pairs={{0,3},{1,4},{2,5},{3,6},{4,7},{5,8},{6,9},{7,10},{8,11},{9,12},{10... | collective-permute-start | bytes 98312 | tf_op jit(solution)/shard_map/ppermute | solution.py:22
  159.6 56.6 %collective-permute-start.13 = (bf16[2,16,512]{2,0,1:T(2,128)(2,1)}, bf16[2,16,512]{2,0,1:T(2,128)(2,1)S(1)}, u32[]{:S(2)}, u32[]{:S(2)}) collective-permute-start(bf16[2,16,512]{2,0,1:T(2,128)(2,1)} %get-tuple-element.12), channel_id=1, source_target_pairs={{0,4},{1,5},{2,6},{3,7},{4,8},{5,9},{6,10},{7,11},{8,12},{9,13},{1... | collective-permute-start | bytes 98312 | tf_op jit(solution)/shard_map/ppermute | solution.py:22
  161.1 6.1 %collective-permute-start.3 = (bf16[2,16,512]{2,0,1:T(2,128)(2,1)}, bf16[2,16,512]{2,0,1:T(2,128)(2,1)S(1)}, u32[]{:S(2)}, u32[]{:S(2)}) collective-permute-start(bf16[2,16,512]{2,0,1:T(2,128)(2,1)} %get-tuple-element.22), channel_id=1, source_target_pairs={{0,14},{1,15},{2,0},{3,1},{4,2},{5,3},{6,4},{7,5},{8,6},{9,7},{10,... | collective-permute-start | bytes 98312 | tf_op jit(solution)/shard_map/ppermute | solution.py:22
  167.1 3.6 %collective-permute-start.4 = (bf16[2,16,512]{2,0,1:T(2,128)(2,1)}, bf16[2,16,512]{2,0,1:T(2,128)(2,1)S(1)}, u32[]{:S(2)}, u32[]{:S(2)}) collective-permute-start(bf16[2,16,512]{2,0,1:T(2,128)(2,1)} %get-tuple-element.21), channel_id=1, source_target_pairs={{0,13},{1,14},{2,15},{3,0},{4,1},{5,2},{6,3},{7,4},{8,5},{9,6},{10... | collective-permute-start | bytes 98312 | tf_op jit(solution)/shard_map/ppermute | solution.py:22
  170.7 4.1 %collective-permute-start.5 = (bf16[2,16,512]{2,0,1:T(2,128)(2,1)}, bf16[2,16,512]{2,0,1:T(2,128)(2,1)S(1)}, u32[]{:S(2)}, u32[]{:S(2)}) collective-permute-start(bf16[2,16,512]{2,0,1:T(2,128)(2,1)} %get-tuple-element.20), channel_id=1, source_target_pairs={{0,12},{1,13},{2,14},{3,15},{4,0},{5,1},{6,2},{7,3},{8,4},{9,5},{1... | collective-permute-start | bytes 98312 | tf_op jit(solution)/shard_map/ppermute | solution.py:22
  174.8 4.5 %collective-permute-start.6 = (bf16[2,16,512]{2,0,1:T(2,128)(2,1)}, bf16[2,16,512]{2,0,1:T(2,128)(2,1)S(1)}, u32[]{:S(2)}, u32[]{:S(2)}) collective-permute-start(bf16[2,16,512]{2,0,1:T(2,128)(2,1)} %get-tuple-element.19), channel_id=1, source_target_pairs={{0,11},{1,12},{2,13},{3,14},{4,15},{5,0},{6,1},{7,2},{8,3},{9,4},{... | collective-permute-start | bytes 98312 | tf_op jit(solution)/shard_map/ppermute | solution.py:22
  179.3 7.1 %collective-permute-start.7 = (bf16[2,16,512]{2,0,1:T(2,128)(2,1)}, bf16[2,16,512]{2,0,1:T(2,128)(2,1)S(1)}, u32[]{:S(2)}, u32[]{:S(2)}) collective-permute-start(bf16[2,16,512]{2,0,1:T(2,128)(2,1)} %get-tuple-element.18), channel_id=1, source_target_pairs={{0,10},{1,11},{2,12},{3,13},{4,14},{5,15},{6,0},{7,1},{8,2},{9,3},... | collective-permute-start | bytes 98312 | tf_op jit(solution)/shard_map/ppermute | solution.py:22
  186.4 5.7 %collective-permute-start.8 = (bf16[2,16,512]{2,0,1:T(2,128)(2,1)}, bf16[2,16,512]{2,0,1:T(2,128)(2,1)S(1)}, u32[]{:S(2)}, u32[]{:S(2)}) collective-permute-start(bf16[2,16,512]{2,0,1:T(2,128)(2,1)} %get-tuple-element.17), channel_id=1, source_target_pairs={{0,9},{1,10},{2,11},{3,12},{4,13},{5,14},{6,15},{7,0},{8,1},{9,2},... | collective-permute-start | bytes 98312 | tf_op jit(solution)/shard_map/ppermute | solution.py:22
  192.1 6.7 %collective-permute-start.9 = (bf16[2,16,512]{2,0,1:T(2,128)(2,1)}, bf16[2,16,512]{2,0,1:T(2,128)(2,1)S(1)}, u32[]{:S(2)}, u32[]{:S(2)}) collective-permute-start(bf16[2,16,512]{2,0,1:T(2,128)(2,1)} %get-tuple-element.16), channel_id=1, source_target_pairs={{0,8},{1,9},{2,10},{3,11},{4,12},{5,13},{6,14},{7,15},{8,0},{9,1},... | collective-permute-start | bytes 98312 | tf_op jit(solution)/shard_map/ppermute | solution.py:22
  198.8 4.6 %collective-permute-start.10 = (bf16[2,16,512]{2,0,1:T(2,128)(2,1)}, bf16[2,16,512]{2,0,1:T(2,128)(2,1)S(1)}, u32[]{:S(2)}, u32[]{:S(2)}) collective-permute-start(bf16[2,16,512]{2,0,1:T(2,128)(2,1)} %get-tuple-element.15), channel_id=1, source_target_pairs={{0,7},{1,8},{2,9},{3,10},{4,11},{5,12},{6,13},{7,14},{8,15},{9,0},... | collective-permute-start | bytes 98312 | tf_op jit(solution)/shard_map/ppermute | solution.py:22
  203.4 7.1 %collective-permute-start.11 = (bf16[2,16,512]{2,0,1:T(2,128)(2,1)}, bf16[2,16,512]{2,0,1:T(2,128)(2,1)S(1)}, u32[]{:S(2)}, u32[]{:S(2)}) collective-permute-start(bf16[2,16,512]{2,0,1:T(2,128)(2,1)} %get-tuple-element.14), channel_id=1, source_target_pairs={{0,6},{1,7},{2,8},{3,9},{4,10},{5,11},{6,12},{7,13},{8,14},{9,15},... | collective-permute-start | bytes 98312 | tf_op jit(solution)/shard_map/ppermute | solution.py:22
  210.5 5.7 %collective-permute-start.12 = (bf16[2,16,512]{2,0,1:T(2,128)(2,1)}, bf16[2,16,512]{2,0,1:T(2,128)(2,1)S(1)}, u32[]{:S(2)}, u32[]{:S(2)}) collective-permute-start(bf16[2,16,512]{2,0,1:T(2,128)(2,1)} %get-tuple-element.13), channel_id=1, source_target_pairs={{0,5},{1,6},{2,7},{3,8},{4,9},{5,10},{6,11},{7,12},{8,13},{9,14},{... | collective-permute-start | bytes 98312 | tf_op jit(solution)/shard_map/ppermute | solution.py:22
  220.8 9.6 %copy-start.14 = (f32[1024]{0:T(1024)S(1)}, f32[1024]{0:T(1024)}, u32[]{:S(2)}) copy-start(f32[1024]{0:T(1024)} %param.17) | copy-start | bytes 12292
  (13 other events, 69.1 us)
